TPU v7x, 512 devices: a whole 4x8x8 slice. The times are simulated.
512 devices in a mesh: dp: 32 (over z, x), tensor: 16 (over y, core).
Axes of the slice: x: 4, y: 8, z: 8, core: 2. Of those that a mesh axis runs over, the one named last changes fastest.
Arguments:
- teacher_hidden: bfloat16 [512, 5120], P('dp', 'tensor'), may hold values from -200 to 200
- student_hidden: bfloat16 [512, 4096], P('dp', 'tensor'), may hold values from -8 to 8
- teacher_head: bfloat16 [5120, 131072], P(None, ('dp', 'tensor')), may hold values from -6 to 6
- student_head: bfloat16 [4096, 131072], P(None, ('dp', 'tensor')), may hold values from -6 to 6
- teacher_gain: float32 [5120], replicated, may hold values from 0.5 to 1.5
- lengths: int32 [64], replicated, may hold values from 1 to 8, as said below
- student_row: int32 [512], replicated, may hold values from 0 to 511, as said below
- targets: int32 [512], replicated, may hold values from 0 to 131071
Outputs:
- grad_logits: bfloat16 [512, 131072], P(None, ('dp', 'tensor'))
- divergence: float32 [512], P('dp')
- log_ratio: float32 [512], P('dp')
Inputs may be any that keep to these rules, and one draw needn't show every extreme that they name: The lengths of the 2 responses of one index of dp sum to at most 8, and to exactly 8 on some index. `student_row`: a permutation: every row of student_hidden is named once.
All inputs are finite; a program needn't handle non-finite values.
Results may differ from a plain program's by a relative error of at most 0.01095.
Values may be sent and summed in bfloat16 or wider, within the bound.
No kernel may reach another device: no remote copies, remote signals or barrier semaphores. Data moves between devices by JAX's collectives and lax.ppermute only.
A program may use at most 64 MiB of HBM per device.

v0:
```python
import functools
import math

import jax
import jax.numpy as jnp
import numpy as np
from jax import lax
from jax.experimental import pallas as pl
from jax.experimental.pallas import tpu as pltpu
from jax.sharding import Mesh
from jax.sharding import PartitionSpec as P


SLOT = 8
LIVE_DEV = 8
DP = ("dp_0", "dp_1")
TENSOR = ("tensor_0", "tensor_1")
DP_TENSOR = ("dp_0", "dp_1", "tensor_0", "tensor_1")


def spread(array, axes):
    count = lax.axis_size(axes)
    return lax.all_to_all(jnp.broadcast_to(array, (count, *array.shape)), axes, 0, 0)


def shifted(array, axis, by):
    count = lax.axis_size(axis)
    return lax.ppermute(array, axis, [(i, (i + by) % count) for i in range(count)])


def ids_of(axes):
    return np.arange(math.prod(lax.axis_size(a) for a in axes)).reshape([lax.axis_size(a) for a in axes])


def stepped(array, by):
    ids = ids_of(DP_TENSOR)
    after = ids.copy()
    after[..., 0] = np.roll(ids[..., 0], -by, axis=2)
    after[..., 1] = np.roll(ids[..., 1], -by, axis=0)
    perm = list(zip(ids.reshape(-1).tolist(), after.reshape(-1).tolist()))
    return lax.ppermute(array, DP_TENSOR, perm)


def plane_groups():
    ids = ids_of(DP_TENSOR)
    zero = ids[..., 0].transpose(2, 0, 1).reshape(ids.shape[2], -1)
    one = ids[..., 1].transpose(0, 2, 1).reshape(ids.shape[0], -1)
    return np.concatenate([zero, one]).tolist()


def ring_pieces(piece, count):
    found = [(0, piece)]
    ahead = behind = piece
    for k in range(1, count // 2):
        ahead = stepped(ahead, 1)
        behind = stepped(behind, -1)
        found += [(-k, ahead), (k, behind)]
    return found + [(-(count // 2), stepped(ahead, 1))]


VMEM = pl.BlockSpec(memory_space=pltpu.VMEM)
SMEM = pl.BlockSpec(memory_space=pltpu.SMEM)


def pick_kernel(lengths, teacher, student, keep, give):
    group = lax.axis_index("dp_0") * lax.axis_size("dp_1") + lax.axis_index("dp_1")
    first, second = lengths[2 * group], lengths[2 * group + 1]
    half, s_width, t_width = student.shape[0] // 2, student.shape[1], teacher.shape[1]
    grid = (LIVE_DEV, teacher.shape[0])
    slot, row = (lax.broadcasted_iota(jnp.int32, grid, d) for d in range(2))
    place = jnp.where(slot < first, slot, SLOT + slot - first)
    pick = jnp.where((place == row) & (slot < first + second), 1.0, 0.0)
    chosen = jnp.dot(
        pick.astype(jnp.bfloat16), teacher[...], preferred_element_type=jnp.float32
    ).astype(jnp.bfloat16)

    def write(students, teachers):
        students[:, :s_width] = student[:half, :]
        students[:, s_width:] = student[half:, :]
        teachers[...] = jnp.zeros(teachers.shape, teachers.dtype)
        teachers[:, :t_width] = chosen

    core = lax.axis_index("tensor_1")
    pl.when(core == 0)(lambda: write(keep, give))
    pl.when(core == 1)(lambda: write(give, keep))


def pack_kernel(s_width, t_width, keep, got, packed):
    core = lax.axis_index("tensor_1")

    @pl.when(core == 0)
    def _():
        for i in range(packed.shape[0]):
            for k, part in enumerate((keep, got)):
                packed[i, :, k * s_width : (k + 1) * s_width] = part[:, :s_width]
                packed[i, :, (2 + k) * s_width : (3 + k) * s_width] = part[:, s_width:]

    @pl.when(core == 1)
    def _():
        for i in range(packed.shape[0]):
            packed[i, :, :t_width] = got[:, :t_width]
            packed[i, :, t_width : 2 * t_width] = keep[:, :t_width]
            packed[i, :, 2 * t_width :] = jnp.zeros(
                (packed.shape[1], packed.shape[2] - 2 * t_width), packed.dtype
            )


def choose_kernel(half, source, gain, everyone, piece, gains):
    count, width = everyone.shape
    s_wide = width // 2
    core = lax.axis_index("tensor_1")
    gains[...] = gain[...]

    @pl.when(core == 0)
    def _():
        j = lax.broadcasted_iota(jnp.int32, (count, count), 1)
        low = (j // half) * (2 * half) + j % half
        want = jnp.broadcast_to(source[:, :1], (count, count))
        one = lambda hit: jnp.where(hit, 1.0, 0.0).astype(jnp.bfloat16)
        dot = functools.partial(jnp.dot, preferred_element_type=jnp.float32)
        chosen = dot(one(want == low), everyone[:, :s_wide])
        chosen += dot(one(want == low + half), everyone[:, s_wide:])
        piece[:, :s_wide] = chosen.astype(jnp.bfloat16)
        piece[:, s_wide:] = jnp.zeros((count, piece.shape[1] - s_wide), piece.dtype)

    @pl.when(core == 1)
    def _():
        piece[...] = everyone[:, : piece.shape[1]]


def block_kernel(offsets, had, s_wide, *refs):
    n = len(offsets)
    blocks, (gains, own, twin), refs = refs[:n], refs[n : n + 3], refs[n + 3 :]
    before, (keep, give, own_buf, twin_buf, sems) = (refs[:2] if had else ()), refs[-5:]
    bufs = (own_buf, twin_buf)

    def fetch(starts, size):
        copies = []
        for i, start in enumerate(starts):
            at = pl.ds(start, size)
            copies.append(
                [
                    pltpu.make_async_copy(head.at[at, :], buf.at[at, :], sems.at[i, k])
                    for k, (head, buf) in enumerate(zip((own, twin), bufs))
                ]
            )
            for copy in copies[-1]:
                copy.start()
        return copies

    rows, t_wide = blocks[0].shape
    dot = functools.partial(jnp.dot, preferred_element_type=jnp.float32)
    core = lax.axis_index("tensor_1")

    @pl.when(core == 0)
    def _():
        y, ys = lax.axis_index("tensor_0"), lax.axis_size("tensor_0")
        totals = [ref[...] for ref in before] if had else [0.0, 0.0]
        starts = [
            pl.multiple_of(lax.rem(y + offset % ys, ys) * s_wide, s_wide) for offset in offsets
        ]
        for block, start, copies in zip(blocks, starts, fetch(starts, s_wide)):
            for copy in copies:
                copy.wait()
            student, features = block[:, :s_wide], pl.ds(start, s_wide)
            totals = [total + dot(student, buf[features, :]) for total, buf in zip(totals, bufs)]
        keep[...], give[...] = totals

    @pl.when(core == 1)
    def _():
        z, zs = lax.axis_index("dp_0"), lax.axis_size("dp_0")
        for k, ref in enumerate((keep, give)):
            ref[...] = before[k][...] if had else jnp.zeros(ref.shape, ref.dtype)
        ys = lax.axis_size("tensor_0")
        copies = fetch([k * t_wide for k in range(ys)], t_wide)
        count = rows // ys
        part = lambda k: jnp.concatenate(
            [block[k * count : (k + 1) * count, :] for block in blocks], axis=0
        ).astype(jnp.float32)
        squares = 0.0
        for k in range(ys):
            values = part(k)
            squares += jnp.sum(values * values, axis=1, keepdims=True)
        row_scale = lax.rsqrt(squares / (ys * t_wide) + 1e-06)
        totals = [0.0, 0.0]
        for k in range(ys):
            normed = (part(k) * row_scale * gains[k : k + 1, :]).astype(jnp.bfloat16)
            for copy in copies[k]:
                copy.wait()
            features = slice(k * t_wide, (k + 1) * t_wide)
            totals = [total + dot(normed, buf[features, :]) for total, buf in zip(totals, bufs)]
        for i, offset in enumerate(offsets):
            at = pl.multiple_of(lax.rem(z + offset % zs, zs) * count, count)
            for ref, total in zip((keep, give), totals):
                ref[pl.ds(at, count), :] = total[i * count : (i + 1) * count, :]


def block_products(found, gains, heads, s_wide, before):
    offsets, blocks = [f[0] for f in found], [f[1] for f in found]
    rows, vocab = blocks[0].shape[0], heads[0].shape[1]
    shape = jax.ShapeDtypeStruct((rows, vocab), jnp.float32)
    return pl.pallas_call(
        functools.partial(block_kernel, offsets, bool(before), s_wide),
        out_shape=(shape, shape),
        in_specs=[VMEM] * (len(blocks) + 1) + [ANY, ANY] + [VMEM] * len(before),
        out_specs=(VMEM, VMEM),
        scratch_shapes=[
            pltpu.VMEM(heads[0].shape, jnp.bfloat16),
            pltpu.VMEM(heads[0].shape, jnp.bfloat16),
            pltpu.SemaphoreType.DMA((lax.axis_size("tensor_0"), 2)),
        ],
        compiler_params=pltpu.CompilerParams(vmem_limit_bytes=LIMIT),
        cost_estimate=pl.CostEstimate(
            flops=4 * len(blocks) * rows * vocab * s_wide,
            bytes_accessed=4 * len(blocks) * vocab * s_wide,
            transcendentals=0,
        ),
    )(*blocks, gains, *heads, *before)


LIMIT = 48 << 20
ANY = pl.BlockSpec(memory_space=pl.ANY)


def merge(parts):
    teacher, student, mean, picked = (parts[:, k] for k in range(4))
    top_t, top_s = jnp.max(teacher, axis=0), jnp.max(student, axis=0)
    sum_t = jnp.sum(jnp.exp(teacher - top_t), axis=0)
    weight = jnp.exp(student - top_s)
    sum_s = jnp.sum(weight, axis=0)
    mean = jnp.sum(weight * mean, axis=0) / sum_s
    return jnp.stack([top_t + jnp.log(sum_t), top_s + jnp.log(sum_s), mean, jnp.sum(picked, axis=0)])


def on_device(
    teacher_hidden,
    student_hidden,
    teacher_head,
    student_head,
    teacher_gain,
    lengths,
    student_row,
    targets,
):
    dp_count = lax.axis_size(DP)
    tensor_count = lax.axis_size(TENSOR)
    y_count, core_count = (lax.axis_size(a) for a in TENSOR)
    local_tokens, t_width = teacher_hidden.shape
    s_width = student_hidden.shape[1]
    token_count = local_tokens * dp_count
    vocab_local = teacher_head.shape[1]
    dp_index = lax.axis_index(DP)
    core = lax.axis_index("tensor_1")
    vocab_start = (dp_index * tensor_count + lax.axis_index(TENSOR)) * vocab_local

    first, second = lengths.reshape(dp_count, 2)[:, :1], lengths.reshape(dp_count, 2)[:, 1:]
    slot = jnp.arange(LIVE_DEV, dtype=jnp.int32)[None, :]
    place = jnp.where(slot < first, slot, SLOT + slot - first)
    live = slot < first + second
    group = jnp.arange(dp_count, dtype=jnp.int32)[:, None] * local_tokens
    row_token = jnp.where(live, group + place, -1).reshape(-1)
    row_live = live.reshape(-1).astype(jnp.float32)
    rows = row_token.shape[0]

    half = local_tokens // 2
    s_wide, t_wide = s_width * core_count, t_width * core_count
    pair = jax.ShapeDtypeStruct((half, 2 * s_width), jnp.bfloat16)
    small = pltpu.CompilerParams(vmem_limit_bytes=8 << 20)
    keep, give = pl.pallas_call(
        pick_kernel,
        out_shape=(pair, pair),
        in_specs=[SMEM, VMEM, VMEM],
        out_specs=(VMEM, VMEM),
        compiler_params=pltpu.CompilerParams(vmem_limit_bytes=62 << 20),
    )(lengths, teacher_hidden, student_hidden)
    packed = pl.pallas_call(
        functools.partial(pack_kernel, s_width, t_width),
        out_shape=jax.ShapeDtypeStruct((dp_count, half, 2 * s_wide), jnp.bfloat16),
        in_specs=[VMEM, VMEM],
        out_specs=VMEM,
        compiler_params=pltpu.CompilerParams(vmem_limit_bytes=62 << 20),
    )(keep, shifted(give, "tensor_1", 1))
    everyone = lax.all_to_all(packed, DP_TENSOR, 0, 0, axis_index_groups=plane_groups())
    tall = jnp.pad(student_head, ((0, t_wide * y_count - s_wide * y_count), (0, 0)))
    away = jnp.where(core == 0, teacher_head, tall)
    own = jnp.where(core == 0, tall, teacher_head)
    heads = (own, shifted(away, "tensor_1", 1))
    gains = teacher_gain.reshape(y_count, t_wide)

    token_of = row_token[:, None] == jnp.arange(token_count, dtype=jnp.int32)[None, :]
    row_source = jnp.sum(jnp.where(token_of, student_row[None, :], 0), axis=1)
    row_target = jnp.sum(jnp.where(token_of, targets[None, :], 0), axis=1)
    piece, gains = pl.pallas_call(
        functools.partial(choose_kernel, half),
        out_shape=(
            jax.ShapeDtypeStruct((rows, t_wide), jnp.bfloat16),
            jax.ShapeDtypeStruct(gains.shape, jnp.float32),
        ),
        in_specs=[VMEM] * 3,
        out_specs=(VMEM, VMEM),
        compiler_params=small,
    )(jnp.broadcast_to(row_source[:, None], (rows, 128)), gains, everyone.reshape(rows, -1))

    found = ring_pieces(piece, y_count)
    parts = block_products(found[:3], gains, heads, s_wide, ())
    parts = block_products(found[3:-1], gains, heads, s_wide, parts)
    kept, sent = block_products(found[-1:], gains, heads, s_wide, parts)
    got = shifted(sent, "tensor_1", 1)
    student_logits = jnp.where(core == 0, kept, got)
    teacher_logits = jnp.where(core == 0, got, kept)

    gap = student_logits - teacher_logits
    hits = (row_target - vocab_start)[:, None] == jnp.arange(vocab_local, dtype=jnp.int32)[None, :]
    picked = jnp.sum(jnp.where(hits, gap, 0.0), axis=1)
    teacher_max = jnp.max(teacher_logits, axis=1)
    student_max = jnp.max(student_logits, axis=1)
    teacher_sum = jnp.sum(jnp.exp(teacher_logits - teacher_max[:, None]), axis=1)
    student_exp = jnp.exp(student_logits - student_max[:, None])
    student_sum = jnp.sum(student_exp, axis=1)
    mean = jnp.sum(student_exp * gap, axis=1) / student_sum
    local = jnp.stack(
        [teacher_max + jnp.log(teacher_sum), student_max + jnp.log(student_sum), mean, picked]
    )
    merged = merge(spread(merge(spread(local, DP)), TENSOR))
    teacher_lse, student_lse, mean, picked = (merged[k] for k in range(4))

    student_prob = jnp.exp(student_logits - student_lse[:, None])
    gradient = (row_live[:, None] * student_prob * (gap - mean[:, None])).astype(jnp.bfloat16)
    lse_gap = teacher_lse - student_lse
    token_ids = jnp.arange(token_count, dtype=jnp.int32)
    unpack = (token_ids[:, None] == row_token[None, :]).astype(jnp.bfloat16)
    grad_logits = jnp.dot(unpack, gradient, preferred_element_type=jnp.float32).astype(jnp.bfloat16)
    own_ids = dp_index * local_tokens + jnp.arange(local_tokens, dtype=jnp.int32)
    own_of = own_ids[:, None] == row_token[None, :]
    divergence = jnp.sum(jnp.where(own_of, (mean + lse_gap)[None, :], 0.0), axis=1)
    log_ratio = jnp.sum(jnp.where(own_of, (picked + lse_gap)[None, :], 0.0), axis=1)
    return (grad_logits, divergence, log_ratio)


def solution(mesh):
    finer = Mesh(mesh.devices.reshape(8, 4, 8, 2), ("dp_0", "dp_1", "tensor_0", "tensor_1"))
    in_specs = (
        P(DP, TENSOR),
        P(DP, TENSOR),
        P(None, DP_TENSOR),
        P(None, DP_TENSOR),
        P(),
        P(),
        P(),
        P(),
    )
    out_specs = (P(None, DP_TENSOR), P(DP), P(DP))
    return jax.shard_map(
        on_device, mesh=finer, in_specs=in_specs, out_specs=out_specs, check_vma=False
    )
```

profile of v0, /device:TPU:1, one launch (start us, length us, event | category | flops | bytes accessed | tf_op | source)
XLA Modules:
  0.0 123.5 jit_solution(15966179987788279422)
XLA Ops:
  0.6 0.0 copy-start.6
  0.7 5.7 %broadcast_select_fusion = (bf16[5120,256]{1,0:T(8,128)(2,1)}, bf16[5120,256]{1,0:T(8,128)(2,1)}) fusion(bf16[5120,256]{1,0:T(8,128)(2,1)} %param.10, pred[]{:T(512)S(6)} %eq.29, bf16[4096,256]{1,0:T(8,128)(2,1)} %param.11), kind=kLoop, calls=%fused_computation | loop fusion | flops 2621440 | bytes 9961473 | tf_op jit(solution)/shard_map/jit(_where)/select_n | solution.py:285
  6.4 8.7 %collective-permute-start.5 = (bf16[5120,256]{1,0:T(8,128)(2,1)}, bf16[5120,256]{1,0:T(8,128)(2,1)}, u32[]{:S(2)}, u32[]{:S(2)}) collective-permute-start(bf16[5120,256]{1,0:T(8,128)(2,1)} %get-tuple-element.52), channel_id=1, source_target_pairs={{0,1},{1,0},{2,3},{3,2},{4,5},{5,4},{6,7},{7,6},{8,9},{9,8},{10,11... | collective-permute-start | bytes 7864328 | tf_op jit(solution)/shard_map/ppermute | solution.py:28
  15.1 1.5 %shard_map.103 = (bf16[8,512]{1,0:T(8,128)(2,1)}, bf16[8,512]{1,0:T(8,128)(2,1)}) custom-call(s32[64]{0:T(128)} %lengths.1, bf16[16,320]{1,0:T(8,128)(2,1)} %teacher.1, bf16[16,256]{1,0:T(8,128)(2,1)} %student.1), custom_call_target="tpu_custom_call" | custom-call | tf_op jit(solution)/shard_map/pallas_call | solution.py:269
  16.6 1.9 %collective-permute-start = (bf16[8,512]{1,0:T(8,128)(2,1)}, bf16[8,512]{1,0:T(8,128)(2,1)S(1)}, u32[]{:S(2)}, u32[]{:S(2)}) collective-permute-start(bf16[8,512]{1,0:T(8,128)(2,1)} %get-tuple-element.14), channel_id=1, source_target_pairs={{0,1},{1,0},{2,3},{3,2},{4,5},{5,4},{6,7},{7,6},{8,9},{9,8},{10,11... | collective-permute-start | bytes 24584 | tf_op jit(solution)/shard_map/ppermute | solution.py:28
  18.5 1.5 %collective-permute-done.got = bf16[8,512]{1,0:T(8,128)(2,1)S(1)} collective-permute-done((bf16[8,512]{1,0:T(8,128)(2,1)}, bf16[8,512]{1,0:T(8,128)(2,1)S(1)}, u32[]{:S(2)}, u32[]{:S(2)}) %collective-permute-start) | collective-permute-done | bytes 8224 | tf_op jit(solution)/shard_map/ppermute | solution.py:28
  20.0 0.6 copy-done.3
  20.6 1.7 %shard_map.104 = bf16[32,8,1024]{2,1,0:T(8,128)(2,1)} custom-call(bf16[8,512]{1,0:T(8,128)(2,1)} %get-tuple-element.13.keep, bf16[8,512]{1,0:T(8,128)(2,1)} %copy-done.3), custom_call_target="tpu_custom_call" | custom-call | tf_op jit(solution)/shard_map/pallas_call | solution.py:276
  22.2 4.3 %all-to-all-start = ((bf16[32,8,1024]{2,1,0:T(8,128)(2,1)}), bf16[32,8,1024]{2,1,0:T(8,128)(2,1)S(1)}, u32[]{:S(2)}, u32[]{:S(2)}) async-start(bf16[32,8,1024]{2,1,0:T(8,128)(2,1)} %shard_map.104), calls=%async_computation | async-start | bytes 1048576 | tf_op jit(solution)/shard_map/all_to_all | solution.py:283
  26.6 0.1 reshape.287
  26.7 0.2 slice_reduce_fusion.2
  26.9 0.1 lt.65
  26.9 0.1 lt.66
  27.0 0.1 lt.63
  27.1 0.1 lt.69
  27.2 0.1 lt.70
  27.3 0.1 add.141
  27.4 0.1 add.142
  27.5 0.1 sub.109
  27.6 0.3 select_reduce_fusion
  27.9 11.3 %all-to-all-done = bf16[32,8,1024]{2,1,0:T(8,128)(2,1)S(1)} async-done(((bf16[32,8,1024]{2,1,0:T(8,128)(2,1)}), bf16[32,8,1024]{2,1,0:T(8,128)(2,1)S(1)}, u32[]{:S(2)}, u32[]{:S(2)}) %all-to-all-start) | async-done | bytes 524320 | tf_op jit(solution)/shard_map/all_to_all | solution.py:283
  39.3 0.1 broadcast_in_dim.83.source
  39.4 4.0 %collective-permute-start.1 = (bf16[256,640]{1,0:T(8,128)(2,1)S(1)}, bf16[256,640]{1,0:T(8,128)(2,1)S(1)}, u32[]{:S(2)}, u32[]{:S(2)}) collective-permute-start(bf16[256,640]{1,0:T(8,128)(2,1)S(1)} %get-tuple-element.15.refs_0_), channel_id=1, source_target_pairs={{0,2},{1,65},{2,4},{3,67},{4,6},{5,69},{6,8},{7,71},{8,10},{9,73},... | collective-permute-start | bytes 983048 | tf_op jit(solution)/shard_map/ppermute | solution.py:41
  43.4 8.6 %collective-permute-start.6 = (bf16[256,640]{1,0:T(8,128)(2,1)S(1)}, bf16[256,640]{1,0:T(8,128)(2,1)S(1)}, u32[]{:S(2)}, u32[]{:S(2)}) collective-permute-start(bf16[256,640]{1,0:T(8,128)(2,1)S(1)} %get-tuple-element.15.refs_0_), channel_id=1, source_target_pairs={{0,14},{1,449},{2,0},{3,451},{4,2},{5,453},{6,4},{7,455},{8,6},{9,... | collective-permute-start | bytes 983048 | tf_op jit(solution)/shard_map/ppermute | solution.py:41
  52.0 2.7 %collective-permute-done.1.refs_1_ = bf16[256,640]{1,0:T(8,128)(2,1)S(1)} collective-permute-done((bf16[256,640]{1,0:T(8,128)(2,1)S(1)}, bf16[256,640]{1,0:T(8,128)(2,1)S(1)}, u32[]{:S(2)}, u32[]{:S(2)}) %collective-permute-start.1) | collective-permute-done | bytes 327712 | tf_op jit(solution)/shard_map/ppermute | solution.py:41
  54.6 1.9 %collective-permute-start.2 = (bf16[256,640]{1,0:T(8,128)(2,1)S(1)}, bf16[256,640]{1,0:T(8,128)(2,1)S(1)}, u32[]{:S(2)}, u32[]{:S(2)}) collective-permute-start(bf16[256,640]{1,0:T(8,128)(2,1)S(1)} %collective-permute-done.1.refs_1_), channel_id=1, source_target_pairs={{0,2},{1,65},{2,4},{3,67},{4,6},{5,69},{6,8},{7,71},{8,10},{9,73},... | collective-permute-start | bytes 983048 | tf_op jit(solution)/shard_map/ppermute | solution.py:41
  56.6 4.6 %collective-permute-start.7 = (bf16[256,640]{1,0:T(8,128)(2,1)S(1)}, bf16[256,640]{1,0:T(8,128)(2,1)S(1)}, u32[]{:S(2)}, u32[]{:S(2)}) collective-permute-start(bf16[256,640]{1,0:T(8,128)(2,1)S(1)} %collective-permute-done.6.refs_2_), channel_id=1, source_target_pairs={{0,14},{1,449},{2,0},{3,451},{4,2},{5,453},{6,4},{7,455},{8,6},{9,... | collective-permute-start | bytes 983048 | tf_op jit(solution)/shard_map/ppermute | solution.py:41
  61.2 2.8 %collective-permute-done.2.refs_0_ = bf16[256,640]{1,0:T(8,128)(2,1)S(1)} collective-permute-done((bf16[256,640]{1,0:T(8,128)(2,1)S(1)}, bf16[256,640]{1,0:T(8,128)(2,1)S(1)}, u32[]{:S(2)}, u32[]{:S(2)}) %collective-permute-start.2) | collective-permute-done | bytes 327712 | tf_op jit(solution)/shard_map/ppermute | solution.py:41
  64.0 1.9 %collective-permute-start.3 = (bf16[256,640]{1,0:T(8,128)(2,1)S(1)}, bf16[256,640]{1,0:T(8,128)(2,1)S(1)}, u32[]{:S(2)}, u32[]{:S(2)}) collective-permute-start(bf16[256,640]{1,0:T(8,128)(2,1)S(1)} %collective-permute-done.2.refs_0_), channel_id=1, source_target_pairs={{0,2},{1,65},{2,4},{3,67},{4,6},{5,69},{6,8},{7,71},{8,10},{9,73},... | collective-permute-start | bytes 983048 | tf_op jit(solution)/shard_map/ppermute | solution.py:41
  65.9 4.6 %collective-permute-start.8 = (bf16[256,640]{1,0:T(8,128)(2,1)S(1)}, bf16[256,640]{1,0:T(8,128)(2,1)S(1)}, u32[]{:S(2)}, u32[]{:S(2)}) collective-permute-start(bf16[256,640]{1,0:T(8,128)(2,1)S(1)} %collective-permute-done.7.refs_1_), channel_id=1, source_target_pairs={{0,14},{1,449},{2,0},{3,451},{4,2},{5,453},{6,4},{7,455},{8,6},{9,... | collective-permute-start | bytes 983048 | tf_op jit(solution)/shard_map/ppermute | solution.py:41
  70.5 2.8 %collective-permute-done.3.refs_2_ = bf16[256,640]{1,0:T(8,128)(2,1)S(1)} collective-permute-done((bf16[256,640]{1,0:T(8,128)(2,1)S(1)}, bf16[256,640]{1,0:T(8,128)(2,1)S(1)}, u32[]{:S(2)}, u32[]{:S(2)}) %collective-permute-start.3) | collective-permute-done | bytes 327712 | tf_op jit(solution)/shard_map/ppermute | solution.py:41
  73.3 1.9 %collective-permute-start.4 = (bf16[256,640]{1,0:T(8,128)(2,1)S(1)}, bf16[256,640]{1,0:T(8,128)(2,1)S(1)}, u32[]{:S(2)}, u32[]{:S(2)}) collective-permute-start(bf16[256,640]{1,0:T(8,128)(2,1)S(1)} %collective-permute-done.3.refs_2_), channel_id=1, source_target_pairs={{0,2},{1,65},{2,4},{3,67},{4,6},{5,69},{6,8},{7,71},{8,10},{9,73},... | collective-permute-start | bytes 983048 | tf_op jit(solution)/shard_map/ppermute | solution.py:41
  75.2 1.7 %copy-done = bf16[5120,256]{1,0:T(8,128)(2,1)S(1)} copy-done((bf16[5120,256]{1,0:T(8,128)(2,1)S(1)}, bf16[5120,256]{1,0:T(8,128)(2,1)}, u32[]{:S(2)}) %copy-start) | copy-done | bytes 2621464
  76.9 2.8 %shard_map.106 = (f32[256,256]{1,0:T(8,128)S(1)}, f32[256,256]{1,0:T(8,128)S(1)}) custom-call(bf16[256,640]{1,0:T(8,128)(2,1)S(1)} %get-tuple-element.15.refs_0_, bf16[256,640]{1,0:T(8,128)(2,1)S(1)} %collective-permute-done.1.refs_1_, bf16[256,640]{1,0:T(8,128)(2,1)S(1)} %collective-permute-done.6.refs_2_, ...), custom_call_target="tpu_custom_call" | custom-call | flops 402653184 | bytes 1572864 | tf_op jit(solution)/shard_map/pallas_call | solution.py:202
  79.7 3.0 %shard_map.107 = (f32[256,256]{1,0:T(8,128)S(1)}, f32[256,256]{1,0:T(8,128)S(1)}) custom-call(bf16[256,640]{1,0:T(8,128)(2,1)S(1)} %collective-permute-done.2.refs_0_, bf16[256,640]{1,0:T(8,128)(2,1)S(1)} %collective-permute-done.7.refs_1_, bf16[256,640]{1,0:T(8,128)(2,1)S(1)} %collective-permute-done.3.refs_2_, ...), custom_call_target="tpu_custom_call" | custom-call | flops 536870912 | bytes 2097152 | tf_op jit(solution)/shard_map/pallas_call | solution.py:202
  82.7 2.5 %shard_map.108 = (f32[256,256]{1,0:T(8,128)S(1)}, f32[256,256]{1,0:T(8,128)S(1)}) custom-call(bf16[256,640]{1,0:T(8,128)(2,1)S(1)} %collective-permute-done.4.refs_0_, f32[8,640]{1,0:T(8,128)S(1)} %get-tuple-element.16.refs_3_.refs_4_.refs_1_, bf16[5120,256]{1,0:T(8,128)(2,1)S(1)} %copy-done.1, ...), custom_call_target="tpu_custom_call" | custom-call | flops 134217728 | bytes 524288 | tf_op jit(solution)/shard_map/pallas_call | solution.py:202
  85.2 3.7 %collective-permute-start.9 = (f32[256,256]{1,0:T(8,128)S(1)}, f32[256,256]{1,0:T(8,128)S(1)}, u32[]{:S(2)}, u32[]{:S(2)}) collective-permute-start(f32[256,256]{1,0:T(8,128)S(1)} %get-tuple-element.22), channel_id=1, source_target_pairs={{0,1},{1,0},{2,3},{3,2},{4,5},{5,4},{6,7},{7,6},{8,9},{9,8},{10,11... | collective-permute-start | bytes 786440 | tf_op jit(solution)/shard_map/ppermute | solution.py:28
  88.9 1.1 collective-permute-done.9
  90.1 0.2 fusion.25
  90.2 0.4 fusion.1
  90.7 14.1 %all_to_all.15 = f32[32,4,256]{2,1,0:T(4,128)S(1)} all-to-all(f32[32,4,256]{2,1,0:T(4,128)S(1)} %broadcast_in_dim.86), channel_id=1, replica_groups=mesh['dp_0'=8,'dp_1'=4,'tensor_0'=8,'tensor_1'=2] {'dp_0','dp_1'}, dimensions={0} | all-to-all | bytes 262144 | tf_op jit(solution)/shard_map/all_to_all | solution.py:23
  104.7 0.1 slice_reduce_fusion.6
  105.0 0.6 broadcast_in_dim.87
  105.6 8.1 %all-to-all-start.2 = ((f32[16,4,256]{2,1,0:T(4,128)}), f32[16,4,256]{2,1,0:T(4,128)S(1)}, u32[]{:S(2)}, u32[]{:S(2)}) async-start(f32[16,4,256]{2,1,0:T(4,128)} %broadcast_in_dim.87), calls=%async_computation.2 | async-start | bytes 131072 | tf_op jit(solution)/shard_map/all_to_all | solution.py:23
  113.7 7.8 %all-to-all-done.2 = f32[16,4,256]{2,1,0:T(4,128)S(1)} async-done(((f32[16,4,256]{2,1,0:T(4,128)}), f32[16,4,256]{2,1,0:T(4,128)S(1)}, u32[]{:S(2)}, u32[]{:S(2)}) %all-to-all-start.2) | async-done | bytes 65568 | tf_op jit(solution)/shard_map/all_to_all | solution.py:23
  121.5 0.1 slice_reduce_fusion.1
  121.7 0.7 fusion.12
  122.4 1.1 convolution_convert_fusion
  (38 shorter events, 0.3 us)
Async XLA Ops:
  0.6 25.9 %copy-start.6 = (s32[64]{0:T(128)S(1)}, s32[64]{0:T(128)}, u32[]{:S(2)}) copy-start(s32[64]{0:T(128)} %lengths.1) | copy-start | bytes 772
  0.7 26.9 %copy-start.2 = (f32[5120]{0:T(1024)S(1)}, f32[5120]{0:T(1024)}, u32[]{:S(2)}) copy-start(f32[5120]{0:T(1024)} %param.12) | copy-start | bytes 61444
  0.7 27.0 %copy-start.4 = (s32[512]{0:T(512)S(1)}, s32[512]{0:T(512)}, u32[]{:S(2)}) copy-start(s32[512]{0:T(512)} %param.15) | copy-start | bytes 6148
  0.7 27.0 %copy-start.5 = (s32[512]{0:T(512)S(1)}, s32[512]{0:T(512)}, u32[]{:S(2)}) copy-start(s32[512]{0:T(512)} %param.14) | copy-start | bytes 6148
  6.4 68.8 %collective-permute-start.5 = (bf16[5120,256]{1,0:T(8,128)(2,1)}, bf16[5120,256]{1,0:T(8,128)(2,1)}, u32[]{:S(2)}, u32[]{:S(2)}) collective-permute-start(bf16[5120,256]{1,0:T(8,128)(2,1)} %get-tuple-element.52), channel_id=1, source_target_pairs={{0,1},{1,0},{2,3},{3,2},{4,5},{5,4},{6,7},{7,6},{8,9},{9,8},{10,11... | collective-permute-start | bytes 7864328 | tf_op jit(solution)/shard_map/ppermute | solution.py:28
  16.6 3.4 %collective-permute-start = (bf16[8,512]{1,0:T(8,128)(2,1)}, bf16[8,512]{1,0:T(8,128)(2,1)S(1)}, u32[]{:S(2)}, u32[]{:S(2)}) collective-permute-start(bf16[8,512]{1,0:T(8,128)(2,1)} %get-tuple-element.14), channel_id=1, source_target_pairs={{0,1},{1,0},{2,3},{3,2},{4,5},{5,4},{6,7},{7,6},{8,9},{9,8},{10,11... | collective-permute-start | bytes 24584 | tf_op jit(solution)/shard_map/ppermute | solution.py:28
  20.0 0.6 copy-start.3
  22.2 17.0 %all-to-all-start = ((bf16[32,8,1024]{2,1,0:T(8,128)(2,1)}), bf16[32,8,1024]{2,1,0:T(8,128)(2,1)S(1)}, u32[]{:S(2)}, u32[]{:S(2)}) async-start(bf16[32,8,1024]{2,1,0:T(8,128)(2,1)} %shard_map.104), calls=%async_computation | async-start | bytes 1048576 | tf_op jit(solution)/shard_map/all_to_all | solution.py:283
  39.4 15.2 %collective-permute-start.1 = (bf16[256,640]{1,0:T(8,128)(2,1)S(1)}, bf16[256,640]{1,0:T(8,128)(2,1)S(1)}, u32[]{:S(2)}, u32[]{:S(2)}) collective-permute-start(bf16[256,640]{1,0:T(8,128)(2,1)S(1)} %get-tuple-element.15.refs_0_), channel_id=1, source_target_pairs={{0,2},{1,65},{2,4},{3,67},{4,6},{5,69},{6,8},{7,71},{8,10},{9,73},... | collective-permute-start | bytes 983048 | tf_op jit(solution)/shard_map/ppermute | solution.py:41
  43.4 13.1 %collective-permute-start.6 = (bf16[256,640]{1,0:T(8,128)(2,1)S(1)}, bf16[256,640]{1,0:T(8,128)(2,1)S(1)}, u32[]{:S(2)}, u32[]{:S(2)}) collective-permute-start(bf16[256,640]{1,0:T(8,128)(2,1)S(1)} %get-tuple-element.15.refs_0_), channel_id=1, source_target_pairs={{0,14},{1,449},{2,0},{3,451},{4,2},{5,453},{6,4},{7,455},{8,6},{9,... | collective-permute-start | bytes 983048 | tf_op jit(solution)/shard_map/ppermute | solution.py:41
  54.6 9.3 %collective-permute-start.2 = (bf16[256,640]{1,0:T(8,128)(2,1)S(1)}, bf16[256,640]{1,0:T(8,128)(2,1)S(1)}, u32[]{:S(2)}, u32[]{:S(2)}) collective-permute-start(bf16[256,640]{1,0:T(8,128)(2,1)S(1)} %collective-permute-done.1.refs_1_), channel_id=1, source_target_pairs={{0,2},{1,65},{2,4},{3,67},{4,6},{5,69},{6,8},{7,71},{8,10},{9,73},... | collective-permute-start | bytes 983048 | tf_op jit(solution)/shard_map/ppermute | solution.py:41
  56.6 9.3 %collective-permute-start.7 = (bf16[256,640]{1,0:T(8,128)(2,1)S(1)}, bf16[256,640]{1,0:T(8,128)(2,1)S(1)}, u32[]{:S(2)}, u32[]{:S(2)}) collective-permute-start(bf16[256,640]{1,0:T(8,128)(2,1)S(1)} %collective-permute-done.6.refs_2_), channel_id=1, source_target_pairs={{0,14},{1,449},{2,0},{3,451},{4,2},{5,453},{6,4},{7,455},{8,6},{9,... | collective-permute-start | bytes 983048 | tf_op jit(solution)/shard_map/ppermute | solution.py:41
  64.0 9.3 %collective-permute-start.3 = (bf16[256,640]{1,0:T(8,128)(2,1)S(1)}, bf16[256,640]{1,0:T(8,128)(2,1)S(1)}, u32[]{:S(2)}, u32[]{:S(2)}) collective-permute-start(bf16[256,640]{1,0:T(8,128)(2,1)S(1)} %collective-permute-done.2.refs_0_), channel_id=1, source_target_pairs={{0,2},{1,65},{2,4},{3,67},{4,6},{5,69},{6,8},{7,71},{8,10},{9,73},... | collective-permute-start | bytes 983048 | tf_op jit(solution)/shard_map/ppermute | solution.py:41
  65.9 13.8 %collective-permute-start.8 = (bf16[256,640]{1,0:T(8,128)(2,1)S(1)}, bf16[256,640]{1,0:T(8,128)(2,1)S(1)}, u32[]{:S(2)}, u32[]{:S(2)}) collective-permute-start(bf16[256,640]{1,0:T(8,128)(2,1)S(1)} %collective-permute-done.7.refs_1_), channel_id=1, source_target_pairs={{0,14},{1,449},{2,0},{3,451},{4,2},{5,453},{6,4},{7,455},{8,6},{9,... | collective-permute-start | bytes 983048 | tf_op jit(solution)/shard_map/ppermute | solution.py:41
  73.3 9.5 %collective-permute-start.4 = (bf16[256,640]{1,0:T(8,128)(2,1)S(1)}, bf16[256,640]{1,0:T(8,128)(2,1)S(1)}, u32[]{:S(2)}, u32[]{:S(2)}) collective-permute-start(bf16[256,640]{1,0:T(8,128)(2,1)S(1)} %collective-permute-done.3.refs_2_), channel_id=1, source_target_pairs={{0,2},{1,65},{2,4},{3,67},{4,6},{5,69},{6,8},{7,71},{8,10},{9,73},... | collective-permute-start | bytes 983048 | tf_op jit(solution)/shard_map/ppermute | solution.py:41
  75.2 1.7 %copy-start = (bf16[5120,256]{1,0:T(8,128)(2,1)S(1)}, bf16[5120,256]{1,0:T(8,128)(2,1)}, u32[]{:S(2)}) copy-start(bf16[5120,256]{1,0:T(8,128)(2,1)} %get-tuple-element.53.refs_4_.refs_5_.refs_2_) | copy-start | bytes 7864324
  76.9 2.8 %copy-start.1 = (bf16[5120,256]{1,0:T(8,128)(2,1)S(1)}, bf16[5120,256]{1,0:T(8,128)(2,1)}, u32[]{:S(2)}) copy-start(bf16[5120,256]{1,0:T(8,128)(2,1)} %get-tuple-element.53.refs_4_.refs_5_.refs_2_) | copy-start | bytes 7864324
  85.2 4.8 %collective-permute-start.9 = (f32[256,256]{1,0:T(8,128)S(1)}, f32[256,256]{1,0:T(8,128)S(1)}, u32[]{:S(2)}, u32[]{:S(2)}) collective-permute-start(f32[256,256]{1,0:T(8,128)S(1)} %get-tuple-element.22), channel_id=1, source_target_pairs={{0,1},{1,0},{2,3},{3,2},{4,5},{5,4},{6,7},{7,6},{8,9},{9,8},{10,11... | collective-permute-start | bytes 786440 | tf_op jit(solution)/shard_map/ppermute | solution.py:28
  105.6 15.9 %all-to-all-start.2 = ((f32[16,4,256]{2,1,0:T(4,128)}), f32[16,4,256]{2,1,0:T(4,128)S(1)}, u32[]{:S(2)}, u32[]{:S(2)}) async-start(f32[16,4,256]{2,1,0:T(4,128)} %broadcast_in_dim.87), calls=%async_computation.2 | async-start | bytes 131072 | tf_op jit(solution)/shard_map/all_to_all | solution.py:23
where the time goes:
time: 124 us; the launch traced here: 123 us
  starting transfers between devices  54.2 us (44%)
  waiting for transfers between devices  30 us (24%)
  blocking collectives  14.1 us (11%)
  Pallas kernels  11.4 us (9%)
  other arithmetic  7.81 us (6%)
  local copies, waits for them, and re-layouts  3.86 us (3%)
    ppermute x7, starting transfers between devices, stepped(): return lax.ppermute(array, DP_TENSOR, perm)  27.4 us
    ppermute x3, starting transfers between devices, shifted(): lax.ppermute(array, axis, [(i, (i + by) % count) for i in range(count)])  14.3 us
    all_to_all x1, blocking collectives, spread(): lax.all_to_all(jnp.broadcast_to(array, (count, *array.shape)), axes, 0, 0)  14.1 us
    all_to_all x1, waiting for transfers between devices, on_device(): lax.all_to_all(packed, DP_TENSOR, 0, 0, axis_index_groups=plane_groups())  11.3 us
    ppermute x7, waiting for transfers between devices, stepped(): return lax.ppermute(array, DP_TENSOR, perm)  8.27 us
    pallas_call x3, Pallas kernels, block_products(): pl.pallas_call(functools.partial(block_kernel, offsets, bool(before), s_w...  8.21 us
    all_to_all x1, starting transfers between devices, spread(): lax.all_to_all(jnp.broadcast_to(array, (count, *array.shape)), axes, 0, 0)  8.13 us
    all_to_all x1, waiting for transfers between devices, spread(): lax.all_to_all(jnp.broadcast_to(array, (count, *array.shape)), axes, 0, 0)  7.77 us
  transfers between devices with their start and end apart: 12, of which 7 were waited for; matrix products, arithmetic and copies ran while one was open for 1% of the time, Pallas kernels for 7%

commit v1 on v0

--- a/solution.py
+++ b/solution.py
@@ -48,14 +48,20 @@
     return np.concatenate([zero, one]).tolist()
 
 
-def ring_pieces(piece, count):
-    found = [(0, piece)]
-    ahead = behind = piece
-    for k in range(1, count // 2):
-        ahead = stepped(ahead, 1)
-        behind = stepped(behind, -1)
-        found += [(-k, ahead), (k, behind)]
-    return found + [(-(count // 2), stepped(ahead, 1))]
+def ring_pieces(piece):
+    ahead_2, behind_2 = stepped(piece, 2), stepped(piece, -2)
+    ahead_1, behind_1 = stepped(piece, 1), stepped(piece, -1)
+    ahead_3, across, behind_3 = stepped(ahead_2, 1), stepped(ahead_2, 2), stepped(behind_2, -1)
+    return [
+        (0, piece),
+        (-1, ahead_1),
+        (1, behind_1),
+        (-2, ahead_2),
+        (2, behind_2),
+        (-3, ahead_3),
+        (3, behind_3),
+        (-4, across),
+    ]
 
 
 VMEM = pl.BlockSpec(memory_space=pltpu.VMEM)
@@ -301,10 +307,9 @@
         compiler_params=small,
     )(jnp.broadcast_to(row_source[:, None], (rows, 128)), gains, everyone.reshape(rows, -1))
 
-    found = ring_pieces(piece, y_count)
-    parts = block_products(found[:3], gains, heads, s_wide, ())
-    parts = block_products(found[3:-1], gains, heads, s_wide, parts)
-    kept, sent = block_products(found[-1:], gains, heads, s_wide, parts)
+    found = ring_pieces(piece)
+    parts = block_products(found[:5], gains, heads, s_wide, ())
+    kept, sent = block_products(found[5:], gains, heads, s_wide, parts)
     got = shifted(sent, "tensor_1", 1)
     student_logits = jnp.where(core == 0, kept, got)
     teacher_logits = jnp.where(core == 0, got, kept)

time: 124 us -> 116 us (0.935)
  waiting for transfers between devices: 30 us -> 22.6 us
  Pallas kernels: 11.4 us -> 9.12 us
  starting transfers between devices: 54.2 us -> 56.4 us
    ppermute x7, waiting for transfers between devices: 8.27 us -> 0.87 us  [stepped(): return lax.ppermute(array, DP_TENSOR, perm)]
    ppermute x3, starting transfers between devices: 14.3 us -> 16.8 us  [shifted(): lax.ppermute(array, axis, [(i, (i + by) % count) for i in range(count)])]
    pallas_call x3 -> x2, Pallas kernels: 8.21 us -> 5.95 us  [block_products(): pl.pallas_call(functools.partial(block_kernel, offsets, bool(before), s_w...]
  transfers between devices with their start and end apart: 12 -> 12, of which waited for: 7 -> 6; matrix products, arithmetic and copies ran while one was open for 1% -> 1% of each run, Pallas kernels for 7% -> 6%
where the time goes in v1:
time: 116 us; the launch traced here: 115 us
  starting transfers between devices  56.4 us (49%)
  waiting for transfers between devices  22.6 us (19%)
  blocking collectives  13.5 us (12%)
  Pallas kernels  9.12 us (8%)
  other arithmetic  7.81 us (7%)
  local copies, waits for them, and re-layouts  3.86 us (3%)
    ppermute x7, starting transfers between devices, stepped(): return lax.ppermute(array, DP_TENSOR, perm)  28 us
    ppermute x3, starting transfers between devices, shifted(): lax.ppermute(array, axis, [(i, (i + by) % count) for i in range(count)])  16.8 us
    all_to_all x1, blocking collectives, spread(): lax.all_to_all(jnp.broadcast_to(array, (count, *array.shape)), axes, 0, 0)  13.5 us
    all_to_all x1, waiting for transfers between devices, on_device(): lax.all_to_all(packed, DP_TENSOR, 0, 0, axis_index_groups=plane_groups())  11.3 us
    all_to_all x1, waiting for transfers between devices, spread(): lax.all_to_all(jnp.broadcast_to(array, (count, *array.shape)), axes, 0, 0)  7.77 us
    all_to_all x1, starting transfers between devices, spread(): lax.all_to_all(jnp.broadcast_to(array, (count, *array.shape)), axes, 0, 0)  7.34 us
    pallas_call x2, Pallas kernels, block_products(): pl.pallas_call(functools.partial(block_kernel, offsets, bool(before), s_w...  5.95 us
    select_n x1, other arithmetic, on_device(): away = jnp.where(core == 0, teacher_head, tall)  5.68 us
  transfers between devices with their start and end apart: 12, of which 6 were waited for; matrix products, arithmetic and copies ran while one was open for 1% of the time, Pallas kernels for 6%

profile of v1, /device:TPU:1, one launch (start us, length us, event | category | flops | bytes accessed | tf_op | source)
XLA Modules:
  0.0 115.4 jit_solution(3396106014724309677)
XLA Ops:
  0.6 0.0 copy-start.6
  0.7 5.7 %broadcast_select_fusion = (bf16[5120,256]{1,0:T(8,128)(2,1)}, bf16[5120,256]{1,0:T(8,128)(2,1)}) fusion(bf16[5120,256]{1,0:T(8,128)(2,1)} %param.10, pred[]{:T(512)S(6)} %eq.29, bf16[4096,256]{1,0:T(8,128)(2,1)} %param.11), kind=kLoop, calls=%fused_computation | loop fusion | flops 2621440 | bytes 9961473 | tf_op jit(solution)/shard_map/jit(_where)/select_n | solution.py:291
  6.4 8.7 %collective-permute-start.6 = (bf16[5120,256]{1,0:T(8,128)(2,1)}, bf16[5120,256]{1,0:T(8,128)(2,1)}, u32[]{:S(2)}, u32[]{:S(2)}) collective-permute-start(bf16[5120,256]{1,0:T(8,128)(2,1)} %get-tuple-element.48), channel_id=1, source_target_pairs={{0,1},{1,0},{2,3},{3,2},{4,5},{5,4},{6,7},{7,6},{8,9},{9,8},{10,11... | collective-permute-start | bytes 7864328 | tf_op jit(solution)/shard_map/ppermute | solution.py:28
  15.1 1.5 %shard_map.103 = (bf16[8,512]{1,0:T(8,128)(2,1)}, bf16[8,512]{1,0:T(8,128)(2,1)}) custom-call(s32[64]{0:T(128)} %lengths.1, bf16[16,320]{1,0:T(8,128)(2,1)} %teacher.1, bf16[16,256]{1,0:T(8,128)(2,1)} %student.1), custom_call_target="tpu_custom_call" | custom-call | tf_op jit(solution)/shard_map/pallas_call | solution.py:275
  16.6 1.9 %collective-permute-start = (bf16[8,512]{1,0:T(8,128)(2,1)}, bf16[8,512]{1,0:T(8,128)(2,1)S(1)}, u32[]{:S(2)}, u32[]{:S(2)}) collective-permute-start(bf16[8,512]{1,0:T(8,128)(2,1)} %get-tuple-element.12), channel_id=1, source_target_pairs={{0,1},{1,0},{2,3},{3,2},{4,5},{5,4},{6,7},{7,6},{8,9},{9,8},{10,11... | collective-permute-start | bytes 24584 | tf_op jit(solution)/shard_map/ppermute | solution.py:28
  18.5 1.5 %collective-permute-done.got = bf16[8,512]{1,0:T(8,128)(2,1)S(1)} collective-permute-done((bf16[8,512]{1,0:T(8,128)(2,1)}, bf16[8,512]{1,0:T(8,128)(2,1)S(1)}, u32[]{:S(2)}, u32[]{:S(2)}) %collective-permute-start) | collective-permute-done | bytes 8224 | tf_op jit(solution)/shard_map/ppermute | solution.py:28
  20.0 0.6 copy-done.3
  20.6 1.7 %shard_map.104 = bf16[32,8,1024]{2,1,0:T(8,128)(2,1)} custom-call(bf16[8,512]{1,0:T(8,128)(2,1)} %get-tuple-element.11.keep, bf16[8,512]{1,0:T(8,128)(2,1)} %copy-done.3), custom_call_target="tpu_custom_call" | custom-call | tf_op jit(solution)/shard_map/pallas_call | solution.py:282
  22.2 4.3 %all-to-all-start = ((bf16[32,8,1024]{2,1,0:T(8,128)(2,1)}), bf16[32,8,1024]{2,1,0:T(8,128)(2,1)S(1)}, u32[]{:S(2)}, u32[]{:S(2)}) async-start(bf16[32,8,1024]{2,1,0:T(8,128)(2,1)} %shard_map.104), calls=%async_computation | async-start | bytes 1048576 | tf_op jit(solution)/shard_map/all_to_all | solution.py:289
  26.6 0.1 reshape.287
  26.7 0.2 slice_reduce_fusion.2
  26.9 0.1 lt.65
  26.9 0.1 lt.66
  27.0 0.1 lt.63
  27.1 0.1 lt.69
  27.2 0.1 lt.70
  27.3 0.1 add.141
  27.4 0.1 add.142
  27.5 0.1 sub.109
  27.6 0.3 select_reduce_fusion
  27.9 11.3 %all-to-all-done = bf16[32,8,1024]{2,1,0:T(8,128)(2,1)S(1)} async-done(((bf16[32,8,1024]{2,1,0:T(8,128)(2,1)}), bf16[32,8,1024]{2,1,0:T(8,128)(2,1)S(1)}, u32[]{:S(2)}, u32[]{:S(2)}) %all-to-all-start) | async-done | bytes 524320 | tf_op jit(solution)/shard_map/all_to_all | solution.py:289
  39.3 0.1 broadcast_in_dim.83.source
  39.4 6.1 %collective-permute-start.1 = (bf16[256,640]{1,0:T(8,128)(2,1)S(1)}, bf16[256,640]{1,0:T(8,128)(2,1)S(1)}, u32[]{:S(2)}, u32[]{:S(2)}) collective-permute-start(bf16[256,640]{1,0:T(8,128)(2,1)S(1)} %get-tuple-element.13.refs_0_), channel_id=1, source_target_pairs={{0,4},{1,129},{2,6},{3,131},{4,8},{5,133},{6,10},{7,135},{8,12},{9... | collective-permute-start | bytes 983048 | tf_op jit(solution)/shard_map/ppermute | solution.py:41
  45.5 6.5 %collective-permute-start.3 = (bf16[256,640]{1,0:T(8,128)(2,1)S(1)}, bf16[256,640]{1,0:T(8,128)(2,1)S(1)}, u32[]{:S(2)}, u32[]{:S(2)}) collective-permute-start(bf16[256,640]{1,0:T(8,128)(2,1)S(1)} %get-tuple-element.13.refs_0_), channel_id=1, source_target_pairs={{0,12},{1,385},{2,14},{3,387},{4,0},{5,389},{6,2},{7,391},{8,4},{9... | collective-permute-start | bytes 983048 | tf_op jit(solution)/shard_map/ppermute | solution.py:41
  52.0 3.1 %collective-permute-start.7 = (bf16[256,640]{1,0:T(8,128)(2,1)S(1)}, bf16[256,640]{1,0:T(8,128)(2,1)S(1)}, u32[]{:S(2)}, u32[]{:S(2)}) collective-permute-start(bf16[256,640]{1,0:T(8,128)(2,1)S(1)} %get-tuple-element.13.refs_0_), channel_id=1, source_target_pairs={{0,2},{1,65},{2,4},{3,67},{4,6},{5,69},{6,8},{7,71},{8,10},{9,73},... | collective-permute-start | bytes 983048 | tf_op jit(solution)/shard_map/ppermute | solution.py:41
  55.1 3.4 %collective-permute-start.8 = (bf16[256,640]{1,0:T(8,128)(2,1)S(1)}, bf16[256,640]{1,0:T(8,128)(2,1)S(1)}, u32[]{:S(2)}, u32[]{:S(2)}) collective-permute-start(bf16[256,640]{1,0:T(8,128)(2,1)S(1)} %get-tuple-element.13.refs_0_), channel_id=1, source_target_pairs={{0,14},{1,449},{2,0},{3,451},{4,2},{5,453},{6,4},{7,455},{8,6},{9,... | collective-permute-start | bytes 983048 | tf_op jit(solution)/shard_map/ppermute | solution.py:41
  58.5 0.0 collective-permute-done.1.refs_3_
  58.5 2.7 %collective-permute-start.2 = (bf16[256,640]{1,0:T(8,128)(2,1)S(1)}, bf16[256,640]{1,0:T(8,128)(2,1)S(1)}, u32[]{:S(2)}, u32[]{:S(2)}) collective-permute-start(bf16[256,640]{1,0:T(8,128)(2,1)S(1)} %collective-permute-done.1.refs_3_), channel_id=1, source_target_pairs={{0,2},{1,65},{2,4},{3,67},{4,6},{5,69},{6,8},{7,71},{8,10},{9,73},... | collective-permute-start | bytes 983048 | tf_op jit(solution)/shard_map/ppermute | solution.py:41
  61.2 3.6 %collective-permute-start.5 = (bf16[256,640]{1,0:T(8,128)(2,1)S(1)}, bf16[256,640]{1,0:T(8,128)(2,1)S(1)}, u32[]{:S(2)}, u32[]{:S(2)}) collective-permute-start(bf16[256,640]{1,0:T(8,128)(2,1)S(1)} %collective-permute-done.1.refs_3_), channel_id=1, source_target_pairs={{0,4},{1,129},{2,6},{3,131},{4,8},{5,133},{6,10},{7,135},{8,12},{9... | collective-permute-start | bytes 983048 | tf_op jit(solution)/shard_map/ppermute | solution.py:41
  64.8 0.0 collective-permute-done.7.refs_1_
  64.8 2.6 %collective-permute-start.4 = (bf16[256,640]{1,0:T(8,128)(2,1)S(1)}, bf16[256,640]{1,0:T(8,128)(2,1)S(1)}, u32[]{:S(2)}, u32[]{:S(2)}) collective-permute-start(bf16[256,640]{1,0:T(8,128)(2,1)S(1)} %collective-permute-done.3.refs_4_), channel_id=1, source_target_pairs={{0,14},{1,449},{2,0},{3,451},{4,2},{5,453},{6,4},{7,455},{8,6},{9,... | collective-permute-start | bytes 983048 | tf_op jit(solution)/shard_map/ppermute | solution.py:41
  67.5 1.7 %copy-done = bf16[5120,256]{1,0:T(8,128)(2,1)S(1)} copy-done((bf16[5120,256]{1,0:T(8,128)(2,1)S(1)}, bf16[5120,256]{1,0:T(8,128)(2,1)}, u32[]{:S(2)}) %copy-start) | copy-done | bytes 2621464
  69.2 3.2 %shard_map.106 = (f32[256,256]{1,0:T(8,128)S(1)}, f32[256,256]{1,0:T(8,128)S(1)}) custom-call(bf16[256,640]{1,0:T(8,128)(2,1)S(1)} %get-tuple-element.13.refs_0_, bf16[256,640]{1,0:T(8,128)(2,1)S(1)} %collective-permute-done.7.refs_1_, bf16[256,640]{1,0:T(8,128)(2,1)S(1)} %collective-permute-done.8.refs_2_, ...), custom_call_target="tpu_custom_call" | custom-call | flops 671088640 | bytes 2621440 | tf_op jit(solution)/shard_map/pallas_call | solution.py:208
  72.5 0.2 collective-permute-done.5.refs_2_
  72.7 0.6 collective-permute-done.4.refs_1_
  73.3 2.7 %shard_map.107 = (f32[256,256]{1,0:T(8,128)S(1)}, f32[256,256]{1,0:T(8,128)S(1)}) custom-call(bf16[256,640]{1,0:T(8,128)(2,1)S(1)} %collective-permute-done.2.refs_0_, bf16[256,640]{1,0:T(8,128)(2,1)S(1)} %collective-permute-done.4.refs_1_, bf16[256,640]{1,0:T(8,128)(2,1)S(1)} %collective-permute-done.5.refs_2_, ...), custom_call_target="tpu_custom_call" | custom-call | flops 402653184 | bytes 1572864 | tf_op jit(solution)/shard_map/pallas_call | solution.py:208
  76.1 6.2 %collective-permute-start.9 = (f32[256,256]{1,0:T(8,128)S(1)}, f32[256,256]{1,0:T(8,128)S(1)}, u32[]{:S(2)}, u32[]{:S(2)}) collective-permute-start(f32[256,256]{1,0:T(8,128)S(1)} %get-tuple-element.18), channel_id=1, source_target_pairs={{0,1},{1,0},{2,3},{3,2},{4,5},{5,4},{6,7},{7,6},{8,9},{9,8},{10,11... | collective-permute-start | bytes 786440 | tf_op jit(solution)/shard_map/ppermute | solution.py:28
  82.3 1.1 collective-permute-done.9
  83.4 0.2 fusion.25
  83.6 0.4 fusion.1
  84.0 13.5 %all_to_all.15 = f32[32,4,256]{2,1,0:T(4,128)S(1)} all-to-all(f32[32,4,256]{2,1,0:T(4,128)S(1)} %broadcast_in_dim.86), channel_id=1, replica_groups=mesh['dp_0'=8,'dp_1'=4,'tensor_0'=8,'tensor_1'=2] {'dp_0','dp_1'}, dimensions={0} | all-to-all | bytes 262144 | tf_op jit(solution)/shard_map/all_to_all | solution.py:23
  97.5 0.1 slice_reduce_fusion.6
  97.7 0.6 broadcast_in_dim.87
  98.4 7.3 %all-to-all-start.2 = ((f32[16,4,256]{2,1,0:T(4,128)}), f32[16,4,256]{2,1,0:T(4,128)S(1)}, u32[]{:S(2)}, u32[]{:S(2)}) async-start(f32[16,4,256]{2,1,0:T(4,128)} %broadcast_in_dim.87), calls=%async_computation.2 | async-start | bytes 131072 | tf_op jit(solution)/shard_map/all_to_all | solution.py:23
  105.7 7.8 %all-to-all-done.2 = f32[16,4,256]{2,1,0:T(4,128)S(1)} async-done(((f32[16,4,256]{2,1,0:T(4,128)}), f32[16,4,256]{2,1,0:T(4,128)S(1)}, u32[]{:S(2)}, u32[]{:S(2)}) %all-to-all-start.2) | async-done | bytes 65568 | tf_op jit(solution)/shard_map/all_to_all | solution.py:23
  113.5 0.1 slice_reduce_fusion.1
  113.6 0.7 fusion.12
  114.3 1.1 convolution_convert_fusion
  (37 shorter events, 0.3 us)
Async XLA Ops:
  0.6 25.9 %copy-start.6 = (s32[64]{0:T(128)S(1)}, s32[64]{0:T(128)}, u32[]{:S(2)}) copy-start(s32[64]{0:T(128)} %lengths.1) | copy-start | bytes 772
  0.7 26.9 %copy-start.2 = (f32[5120]{0:T(1024)S(1)}, f32[5120]{0:T(1024)}, u32[]{:S(2)}) copy-start(f32[5120]{0:T(1024)} %param.12) | copy-start | bytes 61444
  0.7 27.0 %copy-start.4 = (s32[512]{0:T(512)S(1)}, s32[512]{0:T(512)}, u32[]{:S(2)}) copy-start(s32[512]{0:T(512)} %param.15) | copy-start | bytes 6148
  0.7 27.0 %copy-start.5 = (s32[512]{0:T(512)S(1)}, s32[512]{0:T(512)}, u32[]{:S(2)}) copy-start(s32[512]{0:T(512)} %param.14) | copy-start | bytes 6148
  6.4 61.1 %collective-permute-start.6 = (bf16[5120,256]{1,0:T(8,128)(2,1)}, bf16[5120,256]{1,0:T(8,128)(2,1)}, u32[]{:S(2)}, u32[]{:S(2)}) collective-permute-start(bf16[5120,256]{1,0:T(8,128)(2,1)} %get-tuple-element.48), channel_id=1, source_target_pairs={{0,1},{1,0},{2,3},{3,2},{4,5},{5,4},{6,7},{7,6},{8,9},{9,8},{10,11... | collective-permute-start | bytes 7864328 | tf_op jit(solution)/shard_map/ppermute | solution.py:28
  16.6 3.4 %collective-permute-start = (bf16[8,512]{1,0:T(8,128)(2,1)}, bf16[8,512]{1,0:T(8,128)(2,1)S(1)}, u32[]{:S(2)}, u32[]{:S(2)}) collective-permute-start(bf16[8,512]{1,0:T(8,128)(2,1)} %get-tuple-element.12), channel_id=1, source_target_pairs={{0,1},{1,0},{2,3},{3,2},{4,5},{5,4},{6,7},{7,6},{8,9},{9,8},{10,11... | collective-permute-start | bytes 24584 | tf_op jit(solution)/shard_map/ppermute | solution.py:28
  20.0 0.6 copy-start.3
  22.2 17.0 %all-to-all-start = ((bf16[32,8,1024]{2,1,0:T(8,128)(2,1)}), bf16[32,8,1024]{2,1,0:T(8,128)(2,1)S(1)}, u32[]{:S(2)}, u32[]{:S(2)}) async-start(bf16[32,8,1024]{2,1,0:T(8,128)(2,1)} %shard_map.104), calls=%async_computation | async-start | bytes 1048576 | tf_op jit(solution)/shard_map/all_to_all | solution.py:289
  39.4 19.1 %collective-permute-start.1 = (bf16[256,640]{1,0:T(8,128)(2,1)S(1)}, bf16[256,640]{1,0:T(8,128)(2,1)S(1)}, u32[]{:S(2)}, u32[]{:S(2)}) collective-permute-start(bf16[256,640]{1,0:T(8,128)(2,1)S(1)} %get-tuple-element.13.refs_0_), channel_id=1, source_target_pairs={{0,4},{1,129},{2,6},{3,131},{4,8},{5,133},{6,10},{7,135},{8,12},{9... | collective-permute-start | bytes 983048 | tf_op jit(solution)/shard_map/ppermute | solution.py:41
  45.5 15.7 %collective-permute-start.3 = (bf16[256,640]{1,0:T(8,128)(2,1)S(1)}, bf16[256,640]{1,0:T(8,128)(2,1)S(1)}, u32[]{:S(2)}, u32[]{:S(2)}) collective-permute-start(bf16[256,640]{1,0:T(8,128)(2,1)S(1)} %get-tuple-element.13.refs_0_), channel_id=1, source_target_pairs={{0,12},{1,385},{2,14},{3,387},{4,0},{5,389},{6,2},{7,391},{8,4},{9... | collective-permute-start | bytes 983048 | tf_op jit(solution)/shard_map/ppermute | solution.py:41
  52.0 12.8 %collective-permute-start.7 = (bf16[256,640]{1,0:T(8,128)(2,1)S(1)}, bf16[256,640]{1,0:T(8,128)(2,1)S(1)}, u32[]{:S(2)}, u32[]{:S(2)}) collective-permute-start(bf16[256,640]{1,0:T(8,128)(2,1)S(1)} %get-tuple-element.13.refs_0_), channel_id=1, source_target_pairs={{0,2},{1,65},{2,4},{3,67},{4,6},{5,69},{6,8},{7,71},{8,10},{9,73},... | collective-permute-start | bytes 983048 | tf_op jit(solution)/shard_map/ppermute | solution.py:41
  55.1 12.4 %collective-permute-start.8 = (bf16[256,640]{1,0:T(8,128)(2,1)S(1)}, bf16[256,640]{1,0:T(8,128)(2,1)S(1)}, u32[]{:S(2)}, u32[]{:S(2)}) collective-permute-start(bf16[256,640]{1,0:T(8,128)(2,1)S(1)} %get-tuple-element.13.refs_0_), channel_id=1, source_target_pairs={{0,14},{1,449},{2,0},{3,451},{4,2},{5,453},{6,4},{7,455},{8,6},{9,... | collective-permute-start | bytes 983048 | tf_op jit(solution)/shard_map/ppermute | solution.py:41
  58.5 14.0 %collective-permute-start.2 = (bf16[256,640]{1,0:T(8,128)(2,1)S(1)}, bf16[256,640]{1,0:T(8,128)(2,1)S(1)}, u32[]{:S(2)}, u32[]{:S(2)}) collective-permute-start(bf16[256,640]{1,0:T(8,128)(2,1)S(1)} %collective-permute-done.1.refs_3_), channel_id=1, source_target_pairs={{0,2},{1,65},{2,4},{3,67},{4,6},{5,69},{6,8},{7,71},{8,10},{9,73},... | collective-permute-start | bytes 983048 | tf_op jit(solution)/shard_map/ppermute | solution.py:41
  61.2 11.5 %collective-permute-start.5 = (bf16[256,640]{1,0:T(8,128)(2,1)S(1)}, bf16[256,640]{1,0:T(8,128)(2,1)S(1)}, u32[]{:S(2)}, u32[]{:S(2)}) collective-permute-start(bf16[256,640]{1,0:T(8,128)(2,1)S(1)} %collective-permute-done.1.refs_3_), channel_id=1, source_target_pairs={{0,4},{1,129},{2,6},{3,131},{4,8},{5,133},{6,10},{7,135},{8,12},{9... | collective-permute-start | bytes 983048 | tf_op jit(solution)/shard_map/ppermute | solution.py:41
  64.8 8.5 %collective-permute-start.4 = (bf16[256,640]{1,0:T(8,128)(2,1)S(1)}, bf16[256,640]{1,0:T(8,128)(2,1)S(1)}, u32[]{:S(2)}, u32[]{:S(2)}) collective-permute-start(bf16[256,640]{1,0:T(8,128)(2,1)S(1)} %collective-permute-done.3.refs_4_), channel_id=1, source_target_pairs={{0,14},{1,449},{2,0},{3,451},{4,2},{5,453},{6,4},{7,455},{8,6},{9,... | collective-permute-start | bytes 983048 | tf_op jit(solution)/shard_map/ppermute | solution.py:41
  67.5 1.7 %copy-start = (bf16[5120,256]{1,0:T(8,128)(2,1)S(1)}, bf16[5120,256]{1,0:T(8,128)(2,1)}, u32[]{:S(2)}) copy-start(bf16[5120,256]{1,0:T(8,128)(2,1)} %get-tuple-element.49.refs_6_.refs_4_) | copy-start | bytes 7864324
  69.2 4.1 %copy-start.1 = (bf16[5120,256]{1,0:T(8,128)(2,1)S(1)}, bf16[5120,256]{1,0:T(8,128)(2,1)}, u32[]{:S(2)}) copy-start(bf16[5120,256]{1,0:T(8,128)(2,1)} %get-tuple-element.49.refs_6_.refs_4_) | copy-start | bytes 7864324
  76.1 7.3 %collective-permute-start.9 = (f32[256,256]{1,0:T(8,128)S(1)}, f32[256,256]{1,0:T(8,128)S(1)}, u32[]{:S(2)}, u32[]{:S(2)}) collective-permute-start(f32[256,256]{1,0:T(8,128)S(1)} %get-tuple-element.18), channel_id=1, source_target_pairs={{0,1},{1,0},{2,3},{3,2},{4,5},{5,4},{6,7},{7,6},{8,9},{9,8},{10,11... | collective-permute-start | bytes 786440 | tf_op jit(solution)/shard_map/ppermute | solution.py:28
  98.4 15.1 %all-to-all-start.2 = ((f32[16,4,256]{2,1,0:T(4,128)}), f32[16,4,256]{2,1,0:T(4,128)S(1)}, u32[]{:S(2)}, u32[]{:S(2)}) async-start(f32[16,4,256]{2,1,0:T(4,128)} %broadcast_in_dim.87), calls=%async_computation.2 | async-start | bytes 131072 | tf_op jit(solution)/shard_map/all_to_all | solution.py:23

commit v2 on v1

--- a/solution.py
+++ b/solution.py
@@ -326,7 +326,10 @@
     local = jnp.stack(
         [teacher_max + jnp.log(teacher_sum), student_max + jnp.log(student_sum), mean, picked]
     )
-    merged = merge(spread(merge(spread(local, DP)), TENSOR))
+    merged, dp_late = lax.optimization_barrier(
+        (spread(merge(spread(local, DP)), TENSOR), dp_index)
+    )
+    merged = merge(merged)
     teacher_lse, student_lse, mean, picked = (merged[k] for k in range(4))
 
     student_prob = jnp.exp(student_logits - student_lse[:, None])
@@ -335,7 +338,7 @@
     token_ids = jnp.arange(token_count, dtype=jnp.int32)
     unpack = (token_ids[:, None] == row_token[None, :]).astype(jnp.bfloat16)
     grad_logits = jnp.dot(unpack, gradient, preferred_element_type=jnp.float32).astype(jnp.bfloat16)
-    own_ids = dp_index * local_tokens + jnp.arange(local_tokens, dtype=jnp.int32)
+    own_ids = dp_late * local_tokens + jnp.arange(local_tokens, dtype=jnp.int32)
     own_of = own_ids[:, None] == row_token[None, :]
     divergence = jnp.sum(jnp.where(own_of, (mean + lse_gap)[None, :], 0.0), axis=1)
     log_ratio = jnp.sum(jnp.where(own_of, (picked + lse_gap)[None, :], 0.0), axis=1)

time: 116 us -> 115 us (level)
  blocking collectives: 13.5 us -> 28.4 us
  waiting for transfers between devices: 22.6 us -> 14.8 us
  starting transfers between devices: 56.4 us -> 49.1 us
    all_to_all x1 -> x2, blocking collectives: 13.5 us -> 28.4 us  [spread(): lax.all_to_all(jnp.broadcast_to(array, (count, *array.shape)), axes, 0, 0)]
    all_to_all x1 -> x0, waiting for transfers between devices: 7.77 us -> none  [spread(): lax.all_to_all(jnp.broadcast_to(array, (count, *array.shape)), axes, 0, 0)]
    all_to_all x1 -> x0, starting transfers between devices: 7.34 us -> none  [spread(): lax.all_to_all(jnp.broadcast_to(array, (count, *array.shape)), axes, 0, 0)]
  transfers between devices with their start and end apart: 12 -> 11, of which waited for: 6 -> 5; matrix products, arithmetic and copies ran while one was open for 1% -> 1% of each run, Pallas kernels for 6% -> 6%
where the time goes in v2:
time: 115 us
  starting transfers between devices  49.1 us (43%)
  blocking collectives  28.4 us (25%)
  waiting for transfers between devices  14.8 us (13%)
  Pallas kernels  9.12 us (8%)
  other arithmetic  7.82 us (7%)
  local copies, waits for them, and re-layouts  3.25 us (3%)
    all_to_all x2, blocking collectives, spread(): lax.all_to_all(jnp.broadcast_to(array, (count, *array.shape)), axes, 0, 0)  28.4 us
    ppermute x7, starting transfers between devices, stepped(): return lax.ppermute(array, DP_TENSOR, perm)  28 us
    ppermute x3, starting transfers between devices, shifted(): lax.ppermute(array, axis, [(i, (i + by) % count) for i in range(count)])  16.8 us
    all_to_all x1, waiting for transfers between devices, on_device(): lax.all_to_all(packed, DP_TENSOR, 0, 0, axis_index_groups=plane_groups())  11.3 us
    pallas_call x2, Pallas kernels, block_products(): pl.pallas_call(functools.partial(block_kernel, offsets, bool(before), s_w...  5.95 us
    select_n x1, other arithmetic, on_device(): away = jnp.where(core == 0, teacher_head, tall)  5.68 us
    all_to_all x1, starting transfers between devices, on_device(): lax.all_to_all(packed, DP_TENSOR, 0, 0, axis_index_groups=plane_groups())  4.33 us
    ppermute x3, waiting for transfers between devices, shifted(): lax.ppermute(array, axis, [(i, (i + by) % count) for i in range(count)])  2.6 us
  transfers between devices with their start and end apart: 11, of which 5 were waited for; matrix products, arithmetic and copies ran while one was open for 1% of the time, Pallas kernels for 6%

profile of v2, /device:TPU:1, one launch (start us, length us, event | category | flops | bytes accessed | tf_op | source)
XLA Modules:
  0.0 114.6 jit_solution(7718859632260544481)
XLA Ops:
  0.6 0.0 copy-start.6
  0.7 5.7 %broadcast_select_fusion = (bf16[5120,256]{1,0:T(8,128)(2,1)}, bf16[5120,256]{1,0:T(8,128)(2,1)}) fusion(bf16[5120,256]{1,0:T(8,128)(2,1)} %param.10, pred[]{:T(512)S(6)} %eq.29, bf16[4096,256]{1,0:T(8,128)(2,1)} %param.11), kind=kLoop, calls=%fused_computation | loop fusion | flops 2621440 | bytes 9961473 | tf_op jit(solution)/shard_map/jit(_where)/select_n | solution.py:291
  6.4 8.7 %collective-permute-start.6 = (bf16[5120,256]{1,0:T(8,128)(2,1)}, bf16[5120,256]{1,0:T(8,128)(2,1)}, u32[]{:S(2)}, u32[]{:S(2)}) collective-permute-start(bf16[5120,256]{1,0:T(8,128)(2,1)} %get-tuple-element.51), channel_id=1, source_target_pairs={{0,1},{1,0},{2,3},{3,2},{4,5},{5,4},{6,7},{7,6},{8,9},{9,8},{10,11... | collective-permute-start | bytes 7864328 | tf_op jit(solution)/shard_map/ppermute | solution.py:28
  15.1 1.5 %shard_map.103 = (bf16[8,512]{1,0:T(8,128)(2,1)}, bf16[8,512]{1,0:T(8,128)(2,1)}) custom-call(s32[64]{0:T(128)} %lengths.1, bf16[16,320]{1,0:T(8,128)(2,1)} %teacher.1, bf16[16,256]{1,0:T(8,128)(2,1)} %student.1), custom_call_target="tpu_custom_call" | custom-call | tf_op jit(solution)/shard_map/pallas_call | solution.py:275
  16.6 1.9 %collective-permute-start = (bf16[8,512]{1,0:T(8,128)(2,1)}, bf16[8,512]{1,0:T(8,128)(2,1)S(1)}, u32[]{:S(2)}, u32[]{:S(2)}) collective-permute-start(bf16[8,512]{1,0:T(8,128)(2,1)} %get-tuple-element.14), channel_id=1, source_target_pairs={{0,1},{1,0},{2,3},{3,2},{4,5},{5,4},{6,7},{7,6},{8,9},{9,8},{10,11... | collective-permute-start | bytes 24584 | tf_op jit(solution)/shard_map/ppermute | solution.py:28
  18.5 1.5 %collective-permute-done.got = bf16[8,512]{1,0:T(8,128)(2,1)S(1)} collective-permute-done((bf16[8,512]{1,0:T(8,128)(2,1)}, bf16[8,512]{1,0:T(8,128)(2,1)S(1)}, u32[]{:S(2)}, u32[]{:S(2)}) %collective-permute-start) | collective-permute-done | bytes 8224 | tf_op jit(solution)/shard_map/ppermute | solution.py:28
  20.0 0.6 copy-done.3
  20.6 1.7 %shard_map.104 = bf16[32,8,1024]{2,1,0:T(8,128)(2,1)} custom-call(bf16[8,512]{1,0:T(8,128)(2,1)} %get-tuple-element.13.keep, bf16[8,512]{1,0:T(8,128)(2,1)} %copy-done.3), custom_call_target="tpu_custom_call" | custom-call | tf_op jit(solution)/shard_map/pallas_call | solution.py:282
  22.2 4.3 %all-to-all-start = ((bf16[32,8,1024]{2,1,0:T(8,128)(2,1)}), bf16[32,8,1024]{2,1,0:T(8,128)(2,1)S(1)}, u32[]{:S(2)}, u32[]{:S(2)}) async-start(bf16[32,8,1024]{2,1,0:T(8,128)(2,1)} %shard_map.104), calls=%async_computation | async-start | bytes 1048576 | tf_op jit(solution)/shard_map/all_to_all | solution.py:289
  26.6 0.1 reshape.287
  26.7 0.2 slice_reduce_fusion.3
  26.9 0.1 lt.65
  26.9 0.1 lt.66
  27.0 0.1 lt.63
  27.1 0.1 lt.69
  27.2 0.1 lt.70
  27.3 0.1 add.141
  27.4 0.1 add.142
  27.5 0.1 sub.109
  27.6 0.3 select_reduce_fusion
  27.9 11.3 %all-to-all-done = bf16[32,8,1024]{2,1,0:T(8,128)(2,1)S(1)} async-done(((bf16[32,8,1024]{2,1,0:T(8,128)(2,1)}), bf16[32,8,1024]{2,1,0:T(8,128)(2,1)S(1)}, u32[]{:S(2)}, u32[]{:S(2)}) %all-to-all-start) | async-done | bytes 524320 | tf_op jit(solution)/shard_map/all_to_all | solution.py:289
  39.3 0.1 broadcast_in_dim.83.source
  39.4 6.1 %collective-permute-start.1 = (bf16[256,640]{1,0:T(8,128)(2,1)S(1)}, bf16[256,640]{1,0:T(8,128)(2,1)S(1)}, u32[]{:S(2)}, u32[]{:S(2)}) collective-permute-start(bf16[256,640]{1,0:T(8,128)(2,1)S(1)} %get-tuple-element.15.refs_0_), channel_id=1, source_target_pairs={{0,4},{1,129},{2,6},{3,131},{4,8},{5,133},{6,10},{7,135},{8,12},{9... | collective-permute-start | bytes 983048 | tf_op jit(solution)/shard_map/ppermute | solution.py:41
  45.5 6.5 %collective-permute-start.3 = (bf16[256,640]{1,0:T(8,128)(2,1)S(1)}, bf16[256,640]{1,0:T(8,128)(2,1)S(1)}, u32[]{:S(2)}, u32[]{:S(2)}) collective-permute-start(bf16[256,640]{1,0:T(8,128)(2,1)S(1)} %get-tuple-element.15.refs_0_), channel_id=1, source_target_pairs={{0,12},{1,385},{2,14},{3,387},{4,0},{5,389},{6,2},{7,391},{8,4},{9... | collective-permute-start | bytes 983048 | tf_op jit(solution)/shard_map/ppermute | solution.py:41
  52.0 3.1 %collective-permute-start.7 = (bf16[256,640]{1,0:T(8,128)(2,1)S(1)}, bf16[256,640]{1,0:T(8,128)(2,1)S(1)}, u32[]{:S(2)}, u32[]{:S(2)}) collective-permute-start(bf16[256,640]{1,0:T(8,128)(2,1)S(1)} %get-tuple-element.15.refs_0_), channel_id=1, source_target_pairs={{0,2},{1,65},{2,4},{3,67},{4,6},{5,69},{6,8},{7,71},{8,10},{9,73},... | collective-permute-start | bytes 983048 | tf_op jit(solution)/shard_map/ppermute | solution.py:41
  55.1 3.4 %collective-permute-start.8 = (bf16[256,640]{1,0:T(8,128)(2,1)S(1)}, bf16[256,640]{1,0:T(8,128)(2,1)S(1)}, u32[]{:S(2)}, u32[]{:S(2)}) collective-permute-start(bf16[256,640]{1,0:T(8,128)(2,1)S(1)} %get-tuple-element.15.refs_0_), channel_id=1, source_target_pairs={{0,14},{1,449},{2,0},{3,451},{4,2},{5,453},{6,4},{7,455},{8,6},{9,... | collective-permute-start | bytes 983048 | tf_op jit(solution)/shard_map/ppermute | solution.py:41
  58.5 0.0 collective-permute-done.1.refs_3_
  58.5 2.7 %collective-permute-start.2 = (bf16[256,640]{1,0:T(8,128)(2,1)S(1)}, bf16[256,640]{1,0:T(8,128)(2,1)S(1)}, u32[]{:S(2)}, u32[]{:S(2)}) collective-permute-start(bf16[256,640]{1,0:T(8,128)(2,1)S(1)} %collective-permute-done.1.refs_3_), channel_id=1, source_target_pairs={{0,2},{1,65},{2,4},{3,67},{4,6},{5,69},{6,8},{7,71},{8,10},{9,73},... | collective-permute-start | bytes 983048 | tf_op jit(solution)/shard_map/ppermute | solution.py:41
  61.2 0.0 collective-permute-done.3.refs_4_
  61.2 3.6 %collective-permute-start.5 = (bf16[256,640]{1,0:T(8,128)(2,1)S(1)}, bf16[256,640]{1,0:T(8,128)(2,1)S(1)}, u32[]{:S(2)}, u32[]{:S(2)}) collective-permute-start(bf16[256,640]{1,0:T(8,128)(2,1)S(1)} %collective-permute-done.1.refs_3_), channel_id=1, source_target_pairs={{0,4},{1,129},{2,6},{3,131},{4,8},{5,133},{6,10},{7,135},{8,12},{9... | collective-permute-start | bytes 983048 | tf_op jit(solution)/shard_map/ppermute | solution.py:41
  64.8 0.0 collective-permute-done.7.refs_1_
  64.8 2.6 %collective-permute-start.4 = (bf16[256,640]{1,0:T(8,128)(2,1)S(1)}, bf16[256,640]{1,0:T(8,128)(2,1)S(1)}, u32[]{:S(2)}, u32[]{:S(2)}) collective-permute-start(bf16[256,640]{1,0:T(8,128)(2,1)S(1)} %collective-permute-done.3.refs_4_), channel_id=1, source_target_pairs={{0,14},{1,449},{2,0},{3,451},{4,2},{5,453},{6,4},{7,455},{8,6},{9,... | collective-permute-start | bytes 983048 | tf_op jit(solution)/shard_map/ppermute | solution.py:41
  67.5 0.0 collective-permute-done.6.refs_7_.refs_5_
  67.5 1.7 %copy-done = bf16[5120,256]{1,0:T(8,128)(2,1)S(1)} copy-done((bf16[5120,256]{1,0:T(8,128)(2,1)S(1)}, bf16[5120,256]{1,0:T(8,128)(2,1)}, u32[]{:S(2)}) %copy-start) | copy-done | bytes 2621464
  69.2 3.2 %shard_map.106 = (f32[256,256]{1,0:T(8,128)S(1)}, f32[256,256]{1,0:T(8,128)S(1)}) custom-call(bf16[256,640]{1,0:T(8,128)(2,1)S(1)} %get-tuple-element.15.refs_0_, bf16[256,640]{1,0:T(8,128)(2,1)S(1)} %collective-permute-done.7.refs_1_, bf16[256,640]{1,0:T(8,128)(2,1)S(1)} %collective-permute-done.8.refs_2_, ...), custom_call_target="tpu_custom_call" | custom-call | flops 671088640 | bytes 2621440 | tf_op jit(solution)/shard_map/pallas_call | solution.py:208
  72.5 0.2 collective-permute-done.5.refs_2_
  72.7 0.6 collective-permute-done.4.refs_1_
  73.3 2.7 %shard_map.107 = (f32[256,256]{1,0:T(8,128)S(1)}, f32[256,256]{1,0:T(8,128)S(1)}) custom-call(bf16[256,640]{1,0:T(8,128)(2,1)S(1)} %collective-permute-done.2.refs_0_, bf16[256,640]{1,0:T(8,128)(2,1)S(1)} %collective-permute-done.4.refs_1_, bf16[256,640]{1,0:T(8,128)(2,1)S(1)} %collective-permute-done.5.refs_2_, ...), custom_call_target="tpu_custom_call" | custom-call | flops 402653184 | bytes 1572864 | tf_op jit(solution)/shard_map/pallas_call | solution.py:208
  76.1 6.2 %collective-permute-start.9 = (f32[256,256]{1,0:T(8,128)S(1)}, f32[256,256]{1,0:T(8,128)S(1)}, u32[]{:S(2)}, u32[]{:S(2)}) collective-permute-start(f32[256,256]{1,0:T(8,128)S(1)} %get-tuple-element.20), channel_id=1, source_target_pairs={{0,1},{1,0},{2,3},{3,2},{4,5},{5,4},{6,7},{7,6},{8,9},{9,8},{10,11... | collective-permute-start | bytes 786440 | tf_op jit(solution)/shard_map/ppermute | solution.py:28
  82.3 1.1 collective-permute-done.9
  83.4 0.2 fusion.24
  83.6 0.4 fusion.1
  84.0 13.5 %all_to_all.15 = f32[32,4,256]{2,1,0:T(4,128)S(1)} all-to-all(f32[32,4,256]{2,1,0:T(4,128)S(1)} %broadcast_in_dim.86), channel_id=1, replica_groups=mesh['dp_0'=8,'dp_1'=4,'tensor_0'=8,'tensor_1'=2] {'dp_0','dp_1'}, dimensions={0} | all-to-all | bytes 262144 | tf_op jit(solution)/shard_map/all_to_all | solution.py:23
  97.5 0.1 slice_reduce_fusion.6
  97.7 14.9 %all_to_all.16 = f32[16,4,256]{2,1,0:T(4,128)S(1)} all-to-all(f32[16,4,256]{2,1,0:T(4,128)S(1)} %broadcast_in_dim.87), channel_id=1, replica_groups=mesh['dp_0'=8,'dp_1'=4,'tensor_0'=8,'tensor_1'=2] {'tensor_0','tensor_1'}, dimensions={0} | all-to-all | bytes 131072 | tf_op jit(solution)/shard_map/all_to_all | solution.py:23
  112.7 0.1 slice_reduce_fusion.1
  112.8 0.7 fusion.12
  113.5 1.1 convolution_convert_fusion
  (38 shorter events, 0.4 us)
Async XLA Ops:
  0.6 25.9 %copy-start.6 = (s32[64]{0:T(128)S(1)}, s32[64]{0:T(128)}, u32[]{:S(2)}) copy-start(s32[64]{0:T(128)} %lengths.1) | copy-start | bytes 772
  0.7 26.9 %copy-start.2 = (f32[5120]{0:T(1024)S(1)}, f32[5120]{0:T(1024)}, u32[]{:S(2)}) copy-start(f32[5120]{0:T(1024)} %param.12) | copy-start | bytes 61444
  0.7 27.0 %copy-start.4 = (s32[512]{0:T(512)S(1)}, s32[512]{0:T(512)}, u32[]{:S(2)}) copy-start(s32[512]{0:T(512)} %param.15) | copy-start | bytes 6148
  0.7 27.0 %copy-start.5 = (s32[512]{0:T(512)S(1)}, s32[512]{0:T(512)}, u32[]{:S(2)}) copy-start(s32[512]{0:T(512)} %param.14) | copy-start | bytes 6148
  6.4 61.1 %collective-permute-start.6 = (bf16[5120,256]{1,0:T(8,128)(2,1)}, bf16[5120,256]{1,0:T(8,128)(2,1)}, u32[]{:S(2)}, u32[]{:S(2)}) collective-permute-start(bf16[5120,256]{1,0:T(8,128)(2,1)} %get-tuple-element.51), channel_id=1, source_target_pairs={{0,1},{1,0},{2,3},{3,2},{4,5},{5,4},{6,7},{7,6},{8,9},{9,8},{10,11... | collective-permute-start | bytes 7864328 | tf_op jit(solution)/shard_map/ppermute | solution.py:28
  16.6 3.4 %collective-permute-start = (bf16[8,512]{1,0:T(8,128)(2,1)}, bf16[8,512]{1,0:T(8,128)(2,1)S(1)}, u32[]{:S(2)}, u32[]{:S(2)}) collective-permute-start(bf16[8,512]{1,0:T(8,128)(2,1)} %get-tuple-element.14), channel_id=1, source_target_pairs={{0,1},{1,0},{2,3},{3,2},{4,5},{5,4},{6,7},{7,6},{8,9},{9,8},{10,11... | collective-permute-start | bytes 24584 | tf_op jit(solution)/shard_map/ppermute | solution.py:28
  20.0 0.6 copy-start.3
  22.2 17.0 %all-to-all-start = ((bf16[32,8,1024]{2,1,0:T(8,128)(2,1)}), bf16[32,8,1024]{2,1,0:T(8,128)(2,1)S(1)}, u32[]{:S(2)}, u32[]{:S(2)}) async-start(bf16[32,8,1024]{2,1,0:T(8,128)(2,1)} %shard_map.104), calls=%async_computation | async-start | bytes 1048576 | tf_op jit(solution)/shard_map/all_to_all | solution.py:289
  39.4 19.1 %collective-permute-start.1 = (bf16[256,640]{1,0:T(8,128)(2,1)S(1)}, bf16[256,640]{1,0:T(8,128)(2,1)S(1)}, u32[]{:S(2)}, u32[]{:S(2)}) collective-permute-start(bf16[256,640]{1,0:T(8,128)(2,1)S(1)} %get-tuple-element.15.refs_0_), channel_id=1, source_target_pairs={{0,4},{1,129},{2,6},{3,131},{4,8},{5,133},{6,10},{7,135},{8,12},{9... | collective-permute-start | bytes 983048 | tf_op jit(solution)/shard_map/ppermute | solution.py:41
  45.5 15.7 %collective-permute-start.3 = (bf16[256,640]{1,0:T(8,128)(2,1)S(1)}, bf16[256,640]{1,0:T(8,128)(2,1)S(1)}, u32[]{:S(2)}, u32[]{:S(2)}) collective-permute-start(bf16[256,640]{1,0:T(8,128)(2,1)S(1)} %get-tuple-element.15.refs_0_), channel_id=1, source_target_pairs={{0,12},{1,385},{2,14},{3,387},{4,0},{5,389},{6,2},{7,391},{8,4},{9... | collective-permute-start | bytes 983048 | tf_op jit(solution)/shard_map/ppermute | solution.py:41
  52.0 12.8 %collective-permute-start.7 = (bf16[256,640]{1,0:T(8,128)(2,1)S(1)}, bf16[256,640]{1,0:T(8,128)(2,1)S(1)}, u32[]{:S(2)}, u32[]{:S(2)}) collective-permute-start(bf16[256,640]{1,0:T(8,128)(2,1)S(1)} %get-tuple-element.15.refs_0_), channel_id=1, source_target_pairs={{0,2},{1,65},{2,4},{3,67},{4,6},{5,69},{6,8},{7,71},{8,10},{9,73},... | collective-permute-start | bytes 983048 | tf_op jit(solution)/shard_map/ppermute | solution.py:41
  55.1 12.4 %collective-permute-start.8 = (bf16[256,640]{1,0:T(8,128)(2,1)S(1)}, bf16[256,640]{1,0:T(8,128)(2,1)S(1)}, u32[]{:S(2)}, u32[]{:S(2)}) collective-permute-start(bf16[256,640]{1,0:T(8,128)(2,1)S(1)} %get-tuple-element.15.refs_0_), channel_id=1, source_target_pairs={{0,14},{1,449},{2,0},{3,451},{4,2},{5,453},{6,4},{7,455},{8,6},{9,... | collective-permute-start | bytes 983048 | tf_op jit(solution)/shard_map/ppermute | solution.py:41
  58.5 14.0 %collective-permute-start.2 = (bf16[256,640]{1,0:T(8,128)(2,1)S(1)}, bf16[256,640]{1,0:T(8,128)(2,1)S(1)}, u32[]{:S(2)}, u32[]{:S(2)}) collective-permute-start(bf16[256,640]{1,0:T(8,128)(2,1)S(1)} %collective-permute-done.1.refs_3_), channel_id=1, source_target_pairs={{0,2},{1,65},{2,4},{3,67},{4,6},{5,69},{6,8},{7,71},{8,10},{9,73},... | collective-permute-start | bytes 983048 | tf_op jit(solution)/shard_map/ppermute | solution.py:41
  61.2 11.5 %collective-permute-start.5 = (bf16[256,640]{1,0:T(8,128)(2,1)S(1)}, bf16[256,640]{1,0:T(8,128)(2,1)S(1)}, u32[]{:S(2)}, u32[]{:S(2)}) collective-permute-start(bf16[256,640]{1,0:T(8,128)(2,1)S(1)} %collective-permute-done.1.refs_3_), channel_id=1, source_target_pairs={{0,4},{1,129},{2,6},{3,131},{4,8},{5,133},{6,10},{7,135},{8,12},{9... | collective-permute-start | bytes 983048 | tf_op jit(solution)/shard_map/ppermute | solution.py:41
  64.8 8.5 %collective-permute-start.4 = (bf16[256,640]{1,0:T(8,128)(2,1)S(1)}, bf16[256,640]{1,0:T(8,128)(2,1)S(1)}, u32[]{:S(2)}, u32[]{:S(2)}) collective-permute-start(bf16[256,640]{1,0:T(8,128)(2,1)S(1)} %collective-permute-done.3.refs_4_), channel_id=1, source_target_pairs={{0,14},{1,449},{2,0},{3,451},{4,2},{5,453},{6,4},{7,455},{8,6},{9,... | collective-permute-start | bytes 983048 | tf_op jit(solution)/shard_map/ppermute | solution.py:41
  67.5 1.7 %copy-start = (bf16[5120,256]{1,0:T(8,128)(2,1)S(1)}, bf16[5120,256]{1,0:T(8,128)(2,1)}, u32[]{:S(2)}) copy-start(bf16[5120,256]{1,0:T(8,128)(2,1)} %get-tuple-element.52.refs_6_.refs_4_) | copy-start | bytes 7864324
  69.2 4.1 %copy-start.1 = (bf16[5120,256]{1,0:T(8,128)(2,1)S(1)}, bf16[5120,256]{1,0:T(8,128)(2,1)}, u32[]{:S(2)}) copy-start(bf16[5120,256]{1,0:T(8,128)(2,1)} %get-tuple-element.52.refs_6_.refs_4_) | copy-start | bytes 7864324
  76.1 7.3 %collective-permute-start.9 = (f32[256,256]{1,0:T(8,128)S(1)}, f32[256,256]{1,0:T(8,128)S(1)}, u32[]{:S(2)}, u32[]{:S(2)}) collective-permute-start(f32[256,256]{1,0:T(8,128)S(1)} %get-tuple-element.20), channel_id=1, source_target_pairs={{0,1},{1,0},{2,3},{3,2},{4,5},{5,4},{6,7},{7,6},{8,9},{9,8},{10,11... | collective-permute-start | bytes 786440 | tf_op jit(solution)/shard_map/ppermute | solution.py:28
